TPU v7x, 32 devices: a whole 2x2x4 slice. The times are simulated.
32 devices in a mesh: leaf: 4 (over y, x), row: 8 (over z, core).
Axes of the slice: x: 2, y: 2, z: 4, core: 2. Of those that a mesh axis runs over, the one named last changes fastest.
Arguments:
- rhs: bfloat16 [6, 4, 512, 256], P(None, 'leaf', 'row'), may hold values from -6 to 6
- diag_inverse: bfloat16 [4, 6, 512, 512], P('leaf'), as said below
- factor: bfloat16 [4, 58, 512, 512], P('leaf', None, 'row'), as said below
- widths: int32 [6, 4], P(None, 'leaf'), may hold values from 64 to 512, as said below
- structure: int32 [4, 58], P('leaf'), may hold values from 0 to 1, as said below
Outputs:
- forward_solution: bfloat16 [6, 4, 512, 256], P(None, 'leaf', 'row')
- adjoint_solution: bfloat16 [6, 4, 512, 256], P(None, 'leaf', 'row')
Inputs may be any that keep to these rules, and one draw needn't show every extreme that they name: `widths`: every draw has a supernode of exactly 512 columns and one of exactly one eighth of 512 columns. `structure`: 1 where the block is present. Each diag_inverse[j, l] is lower triangular with diagonal entries from 0.5 to 1. `factor`: dense blocks of independent entries.
All inputs are finite; a program needn't handle non-finite values.
Results may differ from a plain program's by a relative error of at most 0.017.
Values may be sent and summed in bfloat16 or wider, within the bound.
No kernel may reach another device: no remote copies, remote signals or barrier semaphores. Data moves between devices by JAX's collectives and lax.ppermute only.
A program may use at most 64 MiB of HBM per device.

v0:
```python
import jax
import jax.numpy as jnp
from jax import lax
from jax.sharding import PartitionSpec as P


def from_partner(x, axis, stride):
    return lax.ppermute(x, axis, [(i, i ^ 1 << stride) for i in range(lax.axis_size(axis))])


def group_size(level_now, leaf_count):
    return min(2**level_now, leaf_count)


def block_offsets(levels, leaf_count):
    offset_table = {}
    cursor = 0
    for source_level in range(levels):
        for target_level in range(source_level + 1, levels):
            offset_table[source_level, target_level] = cursor
            cursor += group_size(target_level, leaf_count)
    return offset_table


def blocks_after(level_now, levels, leaf_count):
    return sum(
        (group_size(target_level, leaf_count) for target_level in range(level_now + 1, levels))
    )


def contract_rows(left_side, right_side):
    return lax.dot_general(
        left_side, right_side, (((0,), (0,)), ((), ())), preferred_element_type=jnp.float32
    )


def apply_columns(matrix, shard_piece):
    return jnp.dot(matrix, shard_piece, preferred_element_type=jnp.float32)


def group_reduce(partials, group_span, leaf_index):
    current = partials
    for bit_number in reversed(range(group_span.bit_length() - 1)):
        half_size = current.shape[0] // 2
        upper_bit = leaf_index // 2**bit_number % 2 == 1
        kept_half = jnp.where(upper_bit, current[half_size:], current[:half_size])
        handed = jnp.where(upper_bit, current[:half_size], current[half_size:])
        current = kept_half + from_partner(handed.astype(jnp.bfloat16), "leaf", bit_number).astype(
            handed.dtype
        )
    return current[0]


def group_collect(own_block, group_span, leaf_index):
    current = own_block[None]
    for bit_number in range(group_span.bit_length() - 1):
        partner = from_partner(current, "leaf", bit_number)
        upper_bit = leaf_index // 2**bit_number % 2 == 1
        current = jnp.where(
            upper_bit,
            jnp.concatenate([partner, current], 0),
            jnp.concatenate([current, partner], 0),
        )
    return current


def adjoint_level(flat_blocks, flat_values, own_full, full_mask, block_mask, inverse_cols):
    pulled = lax.psum(contract_rows(flat_blocks, flat_values).astype(jnp.bfloat16), "row").astype(
        jnp.float32
    )
    reduced_full = (full_mask[:, None] * (own_full.astype(jnp.float32) - pulled)).astype(
        jnp.bfloat16
    )
    solved = contract_rows(inverse_cols, reduced_full)
    return (block_mask[:, None] * solved).astype(jnp.bfloat16)


def shards(rhs, diag_inverse, factor, widths, structure):
    leaf_count = lax.axis_size("leaf")
    leaf_index = lax.axis_index("leaf")
    row_index = lax.axis_index("row")
    levels = rhs.shape[0]
    block_rows = rhs.shape[2]
    columns = rhs.shape[3]
    full_width = factor.shape[3]
    inverse = diag_inverse[0]
    blocks = factor[0]
    weights = structure[0].astype(jnp.float32)
    own_rows = row_index * block_rows
    positions = jnp.arange(full_width, dtype=jnp.int32)
    full_masks = (positions[None, :] < widths).astype(jnp.float32)
    block_masks = lax.dynamic_slice_in_dim(full_masks, own_rows, block_rows, 1)
    offset_table = block_offsets(levels, leaf_count)
    pending = {}
    for target_level in range(1, levels):
        pending[target_level] = jnp.zeros(
            (group_size(target_level, leaf_count), block_rows, columns), jnp.float32
        )
    forward_blocks = []
    forward_full = []
    for level_now in range(levels):
        if level_now > 0:
            incoming = group_reduce(
                pending[level_now], group_size(level_now, leaf_count), leaf_index
            )
        else:
            incoming = jnp.zeros((block_rows, columns), jnp.float32)
        residual = (
            block_masks[level_now][:, None] * (rhs[level_now, 0].astype(jnp.float32) - incoming)
        ).astype(jnp.bfloat16)
        solve_rows = inverse[level_now]
        folded = apply_columns(solve_rows, lax.all_gather(residual, "row", axis=0, tiled=True))
        solved_full = (full_masks[level_now][:, None] * folded).astype(jnp.bfloat16)
        solved_block = lax.dynamic_slice_in_dim(solved_full, own_rows, block_rows, 0)
        forward_blocks.append(solved_block)
        forward_full.append(solved_full)
        if level_now + 1 < levels:
            first_block = offset_table[level_now, level_now + 1]
            block_count = blocks_after(level_now, levels, leaf_count)
            chosen = blocks[first_block : first_block + block_count].reshape(
                block_count * block_rows, full_width
            )
            products = jnp.dot(chosen, solved_full, preferred_element_type=jnp.float32).reshape(
                block_count, block_rows, columns
            )
            products = products * weights[first_block : first_block + block_count][:, None, None]
            cursor = 0
            for target_level in range(level_now + 1, levels):
                group_span = group_size(target_level, leaf_count)
                pending[target_level] = (
                    pending[target_level] + products[cursor : cursor + group_span]
                )
                cursor += group_span
    gathered = {}
    adjoint_blocks = [None] * levels
    for level_now in reversed(range(levels)):
        inverse_cols = lax.dynamic_slice_in_dim(inverse[level_now], own_rows, block_rows, 1)
        if level_now + 1 == levels:
            solved = contract_rows(inverse_cols, forward_full[level_now])
            own_adjoint = (block_masks[level_now][:, None] * solved).astype(jnp.bfloat16)
        else:
            first_block = offset_table[level_now, level_now + 1]
            block_count = blocks_after(level_now, levels, leaf_count)
            stacked = jnp.concatenate(
                [gathered[upper_level] for upper_level in range(level_now + 1, levels)], 0
            )
            stacked = stacked * structure[0, first_block : first_block + block_count][
                :, None, None
            ].astype(jnp.bfloat16)
            flat_blocks = blocks[first_block : first_block + block_count].reshape(
                block_count * block_rows, full_width
            )
            flat_values = stacked.reshape(block_count * block_rows, columns)
            own_adjoint = adjoint_level(
                flat_blocks,
                flat_values,
                forward_full[level_now],
                full_masks[level_now],
                block_masks[level_now],
                inverse_cols,
            )
        adjoint_blocks[level_now] = own_adjoint
        if level_now > 0:
            gathered[level_now] = group_collect(
                own_adjoint, group_size(level_now, leaf_count), leaf_index
            )
    return (jnp.stack(forward_blocks)[:, None], jnp.stack(adjoint_blocks)[:, None])


def solution(mesh):
    placed = (
        P(None, "leaf", "row", None),
        P("leaf", None, None, None),
        P("leaf", None, "row", None),
        P(None, "leaf"),
        P("leaf", None),
    )
    return jax.shard_map(
        shards,
        mesh=mesh,
        in_specs=placed,
        out_specs=(P(None, "leaf", "row", None), P(None, "leaf", "row", None)),
        check_vma=False,
    )
```

profile of v0, /device:TPU:0, one launch (start us, length us, event | category | flops | bytes accessed | tf_op | source)
XLA Modules:
  0.0 502.9 jit_solution(18401244926935718520)
XLA Ops:
  10.1 15.9 %all_gather.18 = bf16[512,256]{1,0:T(8,128)(2,1)S(1)} all-gather(bf16[64,256]{1,0:T(8,128)(2,1)S(1)} %fusion.74), channel_id=1, replica_groups=mesh['leaf'=4,'row'=8] {'row'}, dimensions={0}, use_global_device_ids=true | all-gather | bytes 294912 | tf_op jit(solution)/shard_map/all_gather | solution.py:112
  36.7 14.3 %all_gather.19 = bf16[512,256]{1,0:T(8,128)(2,1)S(1)} all-gather(bf16[64,256]{1,0:T(8,128)(2,1)S(1)} %fusion.73), channel_id=1, replica_groups=mesh['leaf'=4,'row'=8] {'row'}, dimensions={0}, use_global_device_ids=true | all-gather | bytes 294912 | tf_op jit(solution)/shard_map/all_gather | solution.py:112
  54.6 2.5 copy.14
  60.2 2.8 collective-permute-done.1
  67.9 14.2 %all_gather.20 = bf16[512,256]{1,0:T(8,128)(2,1)S(1)} all-gather(bf16[64,256]{1,0:T(8,128)(2,1)S(1)} %fusion.71), channel_id=1, replica_groups=mesh['leaf'=4,'row'=8] {'row'}, dimensions={0}, use_global_device_ids=true | all-gather | bytes 294912 | tf_op jit(solution)/shard_map/all_gather | solution.py:112
  85.5 2.3 copy.15
  90.7 2.8 collective-permute-done.3
  98.4 14.3 %all_gather.21 = bf16[512,256]{1,0:T(8,128)(2,1)S(1)} all-gather(bf16[64,256]{1,0:T(8,128)(2,1)S(1)} %fusion.69), channel_id=1, replica_groups=mesh['leaf'=4,'row'=8] {'row'}, dimensions={0}, use_global_device_ids=true | all-gather | bytes 294912 | tf_op jit(solution)/shard_map/all_gather | solution.py:112
  121.1 2.8 collective-permute-done.5
  128.8 14.2 %all_gather.22 = bf16[512,256]{1,0:T(8,128)(2,1)S(1)} all-gather(bf16[64,256]{1,0:T(8,128)(2,1)S(1)} %fusion.67), channel_id=1, replica_groups=mesh['leaf'=4,'row'=8] {'row'}, dimensions={0}, use_global_device_ids=true | all-gather | bytes 294912 | tf_op jit(solution)/shard_map/all_gather | solution.py:112
  147.5 2.7 collective-permute-done.7
  155.2 14.3 %all_gather.23 = bf16[512,256]{1,0:T(8,128)(2,1)S(1)} all-gather(bf16[64,256]{1,0:T(8,128)(2,1)S(1)} %fusion.65), channel_id=1, replica_groups=mesh['leaf'=4,'row'=8] {'row'}, dimensions={0}, use_global_device_ids=true | all-gather | bytes 294912 | tf_op jit(solution)/shard_map/all_gather | solution.py:112
  171.7 2.4 collective-permute-done.9
  175.9 2.6 collective-permute-done.10
  179.6 56.5 %all-reduce.6.cloned.1.call-done = bf16[512,256]{0,1:T(8,128)(2,1)} async-done(((bf16[512,256]{0,1:T(8,128)(2,1)}), bf16[512,256]{0,1:T(8,128)(2,1)}) %all-reduce.6.cloned.1.call-update) | async-done | bytes 262160 | tf_op jit(solution)/shard_map/psum | solution.py:68
  239.0 2.4 collective-permute-done.11
  243.0 2.7 collective-permute-done.12
  247.0 54.6 %all-reduce.8.cloned.1.call-done = bf16[512,256]{0,1:T(8,128)(2,1)} async-done(((bf16[512,256]{0,1:T(8,128)(2,1)}), bf16[512,256]{0,1:T(8,128)(2,1)}) %all-reduce.8.cloned.1.call-update) | async-done | bytes 262160 | tf_op jit(solution)/shard_map/psum | solution.py:68
  304.5 2.4 collective-permute-done.13
  308.5 2.7 collective-permute-done.14
  312.6 54.5 %all-reduce.10.cloned.1.call-done = bf16[512,256]{0,1:T(8,128)(2,1)} async-done(((bf16[512,256]{0,1:T(8,128)(2,1)}), bf16[512,256]{0,1:T(8,128)(2,1)}) %all-reduce.10.cloned.1.call-update) | async-done | bytes 262160 | tf_op jit(solution)/shard_map/psum | solution.py:68
  370.0 2.4 collective-permute-done.15
  379.6 53.1 %all-reduce.12.cloned.1.call-done = bf16[512,256]{0,1:T(8,128)(2,1)} async-done(((bf16[512,256]{0,1:T(8,128)(2,1)}), bf16[512,256]{0,1:T(8,128)(2,1)}) %all-reduce.12.cloned.1.call-update) | async-done | bytes 262160 | tf_op jit(solution)/shard_map/psum | solution.py:68
  442.4 51.9 %all-reduce.14.cloned.1.call-done = bf16[512,256]{0,1:T(8,128)(2,1)} async-done(((bf16[512,256]{0,1:T(8,128)(2,1)}), bf16[512,256]{0,1:T(8,128)(2,1)}) %all-reduce.14.cloned.1.call-update) | async-done | bytes 262160 | tf_op jit(solution)/shard_map/psum | solution.py:68
  (220 shorter events, 96.6 us)
Async XLA Ops:
  7.2 229.0 %all-reduce.6.cloned.1.call-start = ((), (), s32[]{:S(2)}) async-start(), calls=%async_computation | async-start | bytes 524288 | tf_op jit(solution)/shard_map/psum | solution.py:68
  31.9 4.0 collective-permute-start
  58.6 4.4 collective-permute-start.1
  63.1 4.0 collective-permute-start.2
  89.1 4.4 collective-permute-start.3
  93.6 4.0 collective-permute-start.4
  119.5 4.4 collective-permute-start.5
  123.9 4.0 collective-permute-start.6
  144.5 91.6 %copy-start.14 = (bf16[256,512]{1,0:T(8,128)(2,1)}, bf16[256,512]{1,0:T(8,128)(2,1)S(1)}, u32[]{:S(2)}) copy-start(bf16[256,512]{1,0:T(8,128)(2,1)S(1)} %fusion.4) | copy-start | bytes 786436
  145.9 4.4 collective-permute-start.7
  150.4 4.0 collective-permute-start.8
  170.2 4.0 collective-permute-start.9
  174.2 4.3 collective-permute-start.10
  179.6 122.0 %all-reduce.8.cloned.1.call-start = ((), (), s32[]{:S(2)}) async-start(), calls=%async_computation.1 | async-start | bytes 524288 | tf_op jit(solution)/shard_map/psum | solution.py:68
  237.4 4.0 collective-permute-start.11
  241.4 4.3 collective-permute-start.12
  247.0 120.2 %all-reduce.10.cloned.1.call-start = ((), (), s32[]{:S(2)}) async-start(), calls=%async_computation.2 | async-start | bytes 524288 | tf_op jit(solution)/shard_map/psum | solution.py:68
  302.9 4.0 collective-permute-start.13
  306.9 4.3 collective-permute-start.14
  312.5 120.3 %all-reduce.12.cloned.1.call-start = ((), (), s32[]{:S(2)}) async-start(), calls=%async_computation.3 | async-start | bytes 524288 | tf_op jit(solution)/shard_map/psum | solution.py:68
  368.5 4.0 collective-permute-start.15
  372.5 4.3 collective-permute-start.16
  378.2 116.1 %all-reduce.14.cloned.1.call-start = ((), (), s32[]{:S(2)}) async-start(), calls=%async_computation.4 | async-start | bytes 524288 | tf_op jit(solution)/shard_map/psum | solution.py:68
  434.1 4.0 collective-permute-start.17
  (41 other events, 1000.0 us)
Sparse Core Ops, SparseCore 0:
  179.7 56.4 all-reduce.5
  247.1 54.4 all-reduce.7
  312.6 54.4 all-reduce.9
  378.3 54.4 all-reduce.11
  439.8 54.4 all-reduce.13
where the time goes:
time: 504 us; the launch traced here: 503 us
  waiting for transfers between devices  308 us (61%)
  blocking collectives  87.2 us (17%)
  starting transfers between devices  28.5 us (6%)
  local copies, waits for them, and re-layouts  26.8 us (5%)
  matrix products  24.5 us (5%)
  between operations  14.7 us (3%)
  other arithmetic  12.9 us (3%)
    psum x5, waiting for transfers between devices, adjoint_level(): lax.psum(contract_rows(flat_blocks, flat_values).astype(jnp.bfloat16), 'r...  271 us
    all_gather x6, blocking collectives, shards(): lax.all_gather(residual, 'row', axis=0, tiled=True)  87.2 us
    ppermute x18, waiting for transfers between devices, from_partner(): lax.ppermute(x, axis, [(i, i ^ 1 << stride) for i in range(lax.axis_size(...  37.7 us
    ppermute x18, starting transfers between devices, from_partner(): lax.ppermute(x, axis, [(i, i ^ 1 << stride) for i in range(lax.axis_size(...  28.2 us
    dot_general x11, matrix products, contract_rows(): lax.dot_general(left_side, right_side, (((0,), (0,)), ((), ())), preferre...  12.3 us
    unnamed x97, local copies, waits for them, and re-layouts  10.3 us
  transfers between devices with their start and end apart: 23, of which 23 were waited for; matrix products, arithmetic and copies ran while one was open for 3% of the time, Pallas kernels for 0%

commit v1 on v0

--- a/solution.py
+++ b/solution.py
@@ -2,6 +2,12 @@
 import jax.numpy as jnp
 from jax import lax
 from jax.sharding import PartitionSpec as P
+
+
+def summed_here(x, name):
+    parts = lax.all_gather(x, name, axis=0, tiled=False)
+    summed = parts.sum(axis=0)
+    return summed
 
 
 def from_partner(x, axis, stride):
@@ -65,9 +71,9 @@
 
 
 def adjoint_level(flat_blocks, flat_values, own_full, full_mask, block_mask, inverse_cols):
-    pulled = lax.psum(contract_rows(flat_blocks, flat_values).astype(jnp.bfloat16), "row").astype(
-        jnp.float32
-    )
+    pulled = summed_here(
+        contract_rows(flat_blocks, flat_values).astype(jnp.bfloat16), "row"
+    ).astype(jnp.float32)
     reduced_full = (full_mask[:, None] * (own_full.astype(jnp.float32) - pulled)).astype(
         jnp.bfloat16
     )

time: 504 us -> 393 us (0.78)
  waiting for transfers between devices: 308 us -> 183 us
  other arithmetic: 12.9 us -> 21.6 us
  local copies, waits for them, and re-layouts: 26.8 us -> 34.2 us
    psum x5 -> x0, waiting for transfers between devices: 271 us -> none  [adjoint_level(): lax.psum(contract_rows(flat_blocks, flat_values).astype(jnp.bfloat16), 'r...]
    all_gather x0 -> x5, waiting for transfers between devices: none -> 143 us  [summed_here(): parts = lax.all_gather(x, name, axis=0, tiled=False)]
    reduce_sum x0 -> x5, other arithmetic: none -> 7.77 us  [summed_here(): summed = parts.sum(axis=0)]
    unnamed x97 -> x78, local copies, waits for them, and re-layouts: 10.3 us -> 17.9 us
  transfers between devices with their start and end apart: 23 -> 23, of which waited for: 23 -> 23; matrix products, arithmetic and copies ran while one was open for 3% -> 2% of each run, Pallas kernels for 0% -> 0%
where the time goes in v1:
time: 393 us; the launch traced here: 391 us
  waiting for transfers between devices  183 us (47%)
  blocking collectives  87.3 us (22%)
  local copies, waits for them, and re-layouts  34.2 us (9%)
  starting transfers between devices  28.5 us (7%)
  matrix products  21.8 us (6%)
  other arithmetic  21.6 us (5%)
  between operations  14.6 us (4%)
    all_gather x5, waiting for transfers between devices, summed_here(): parts = lax.all_gather(x, name, axis=0, tiled=False)  143 us
    all_gather x6, blocking collectives, shards(): lax.all_gather(residual, 'row', axis=0, tiled=True)  87.3 us
    ppermute x18, waiting for transfers between devices, from_partner(): lax.ppermute(x, axis, [(i, i ^ 1 << stride) for i in range(lax.axis_size(...  40.2 us
    ppermute x18, starting transfers between devices, from_partner(): lax.ppermute(x, axis, [(i, i ^ 1 << stride) for i in range(lax.axis_size(...  27.9 us
    unnamed x78, local copies, waits for them, and re-layouts  17.9 us
    dot_general x11, matrix products, contract_rows(): lax.dot_general(left_side, right_side, (((0,), (0,)), ((), ())), preferre...  10.9 us
  transfers between devices with their start and end apart: 23, of which 23 were waited for; matrix products, arithmetic and copies ran while one was open for 2% of the time, Pallas kernels for 0%

profile of v1, /device:TPU:0, one launch (start us, length us, event | category | flops | bytes accessed | tf_op | source)
XLA Modules:
  0.0 391.2 jit_solution(15593401279853406098)
XLA Ops:
  10.1 15.9 %all_gather.48 = bf16[512,256]{1,0:T(8,128)(2,1)S(1)} all-gather(bf16[64,256]{1,0:T(8,128)(2,1)S(1)} %fusion.74), channel_id=1, replica_groups=mesh['leaf'=4,'row'=8] {'row'}, dimensions={0}, use_global_device_ids=true | all-gather | bytes 294912 | tf_op jit(solution)/shard_map/all_gather | solution.py:118
  38.5 14.3 %all_gather.49 = bf16[512,256]{1,0:T(8,128)(2,1)S(1)} all-gather(bf16[64,256]{1,0:T(8,128)(2,1)S(1)} %fusion.73), channel_id=1, replica_groups=mesh['leaf'=4,'row'=8] {'row'}, dimensions={0}, use_global_device_ids=true | all-gather | bytes 294912 | tf_op jit(solution)/shard_map/all_gather | solution.py:118
  56.4 2.5 copy.14
  61.9 2.8 collective-permute-done.1
  69.6 14.2 %all_gather.50 = bf16[512,256]{1,0:T(8,128)(2,1)S(1)} all-gather(bf16[64,256]{1,0:T(8,128)(2,1)S(1)} %fusion.71), channel_id=1, replica_groups=mesh['leaf'=4,'row'=8] {'row'}, dimensions={0}, use_global_device_ids=true | all-gather | bytes 294912 | tf_op jit(solution)/shard_map/all_gather | solution.py:118
  92.5 2.8 collective-permute-done.3
  100.2 14.3 %all_gather.51 = bf16[512,256]{1,0:T(8,128)(2,1)S(1)} all-gather(bf16[64,256]{1,0:T(8,128)(2,1)S(1)} %fusion.69), channel_id=1, replica_groups=mesh['leaf'=4,'row'=8] {'row'}, dimensions={0}, use_global_device_ids=true | all-gather | bytes 294912 | tf_op jit(solution)/shard_map/all_gather | solution.py:118
  121.9 2.8 collective-permute-done.5
  129.6 14.3 %all_gather.52 = bf16[512,256]{1,0:T(8,128)(2,1)S(1)} all-gather(bf16[64,256]{1,0:T(8,128)(2,1)S(1)} %fusion.67), channel_id=1, replica_groups=mesh['leaf'=4,'row'=8] {'row'}, dimensions={0}, use_global_device_ids=true | all-gather | bytes 294912 | tf_op jit(solution)/shard_map/all_gather | solution.py:118
  147.2 2.9 collective-permute-done.7
  155.0 14.3 %all_gather.53 = bf16[512,256]{1,0:T(8,128)(2,1)S(1)} all-gather(bf16[64,256]{1,0:T(8,128)(2,1)S(1)} %fusion.65), channel_id=1, replica_groups=mesh['leaf'=4,'row'=8] {'row'}, dimensions={0}, use_global_device_ids=true | all-gather | bytes 294912 | tf_op jit(solution)/shard_map/all_gather | solution.py:118
  175.5 2.7 collective-permute-done.10
  179.6 30.0 %all-gather.11.cloned.1.call-done = bf16[4096,256]{0,1:T(8,128)(2,1)} async-done(((bf16[512,256]{0,1:T(8,128)(2,1)}), bf16[4096,256]{0,1:T(8,128)(2,1)}) %all-gather.11.cloned.1.call-update) | async-done | bytes 2097168 | tf_op jit(solution)/shard_map/all_gather | solution.py:8
  209.5 2.5 copy.19
  219.5 2.7 collective-permute-done.12
  223.4 28.7 %all-gather.13.cloned.1.call-done = bf16[4096,256]{0,1:T(8,128)(2,1)} async-done(((bf16[512,256]{0,1:T(8,128)(2,1)}), bf16[4096,256]{0,1:T(8,128)(2,1)}) %all-gather.13.cloned.1.call-update) | async-done | bytes 2097168 | tf_op jit(solution)/shard_map/all_gather | solution.py:8
  252.1 2.5 copy.20
  263.0 2.7 collective-permute-done.14
  267.0 28.7 %all-gather.15.cloned.1.call-done = bf16[4096,256]{0,1:T(8,128)(2,1)} async-done(((bf16[512,256]{0,1:T(8,128)(2,1)}), bf16[4096,256]{0,1:T(8,128)(2,1)}) %all-gather.15.cloned.1.call-update) | async-done | bytes 2097168 | tf_op jit(solution)/shard_map/all_gather | solution.py:8
  295.6 2.5 copy.21
  306.5 2.7 collective-permute-done.16
  310.8 28.4 %all-gather.17.cloned.1.call-done = bf16[4096,256]{0,1:T(8,128)(2,1)} async-done(((bf16[512,256]{0,1:T(8,128)(2,1)}), bf16[4096,256]{0,1:T(8,128)(2,1)}) %all-gather.17.cloned.1.call-update) | async-done | bytes 2097168 | tf_op jit(solution)/shard_map/all_gather | solution.py:8
  339.3 2.5 copy.22
  351.5 27.2 %all-gather.19.cloned.1.call-done = bf16[4096,256]{0,1:T(8,128)(2,1)} async-done(((bf16[512,256]{0,1:T(8,128)(2,1)}), bf16[4096,256]{0,1:T(8,128)(2,1)}) %all-gather.19.cloned.1.call-update) | async-done | bytes 2097168 | tf_op jit(solution)/shard_map/all_gather | solution.py:8
  (206 shorter events, 111.7 us)
Async XLA Ops:
  7.2 202.4 %all-gather.11.cloned.1.call-start = ((), (), s32[]{:S(2)}) async-start(), calls=%async_computation | async-start | bytes 2359296 | tf_op jit(solution)/shard_map/all_gather | solution.py:8
  33.7 4.0 %collective-permute-start = (bf16[1,64,256]{2,1,0:T(8,128)(2,1)S(1)}, bf16[1,64,256]{2,1,0:T(8,128)(2,1)S(1)}, u32[]{:S(2)}, u32[]{:S(2)}) collective-permute-start(bf16[1,64,256]{2,1,0:T(8,128)(2,1)S(1)} %select_convert_fusion.8), channel_id=1, source_target_pairs={{0,8},{8,0},{16,24},{24,16},{1,9},{9,1},{17,25},{25,17},{2,10},{10... | collective-permute-start | bytes 98312 | tf_op jit(solution)/shard_map/ppermute | solution.py:14
  60.3 30.5 %copy-start = (f32[16,64,256]{2,1,0:T(8,128)}, f32[16,64,256]{2,1,0:T(8,128)S(1)}, u32[]{:S(2)}) copy-start(f32[16,64,256]{2,1,0:T(8,128)S(1)} %broadcast_multiply_fusion.1) | copy-start | bytes 3145732
  60.4 4.4 %collective-permute-start.1 = (bf16[2,64,256]{2,1,0:T(8,128)(2,1)S(1)}, bf16[2,64,256]{2,1,0:T(8,128)(2,1)S(1)}, u32[]{:S(2)}, u32[]{:S(2)}) collective-permute-start(bf16[2,64,256]{2,1,0:T(8,128)(2,1)S(1)} %select_convert_fusion.3), channel_id=1, source_target_pairs={{0,16},{8,24},{16,0},{24,8},{1,17},{9,25},{17,1},{25,9},{2,18},{10... | collective-permute-start | bytes 196616 | tf_op jit(solution)/shard_map/ppermute | solution.py:14
  64.8 4.0 %collective-permute-start.2 = (bf16[1,64,256]{2,1,0:T(8,128)(2,1)S(1)}, bf16[1,64,256]{2,1,0:T(8,128)(2,1)S(1)}, u32[]{:S(2)}, u32[]{:S(2)}) collective-permute-start(bf16[1,64,256]{2,1,0:T(8,128)(2,1)S(1)} %select_convert_fusion.7), channel_id=1, source_target_pairs={{0,8},{8,0},{16,24},{24,16},{1,9},{9,1},{17,25},{25,17},{2,10},{10... | collective-permute-start | bytes 98312 | tf_op jit(solution)/shard_map/ppermute | solution.py:14
  90.9 4.4 %collective-permute-start.3 = (bf16[2,64,256]{2,1,0:T(8,128)(2,1)S(1)}, bf16[2,64,256]{2,1,0:T(8,128)(2,1)S(1)}, u32[]{:S(2)}, u32[]{:S(2)}) collective-permute-start(bf16[2,64,256]{2,1,0:T(8,128)(2,1)S(1)} %select_convert_fusion.2), channel_id=1, source_target_pairs={{0,16},{8,24},{16,0},{24,8},{1,17},{9,25},{17,1},{25,9},{2,18},{10... | collective-permute-start | bytes 196616 | tf_op jit(solution)/shard_map/ppermute | solution.py:14
  95.3 4.0 %collective-permute-start.4 = (bf16[1,64,256]{2,1,0:T(8,128)(2,1)S(1)}, bf16[1,64,256]{2,1,0:T(8,128)(2,1)S(1)}, u32[]{:S(2)}, u32[]{:S(2)}) collective-permute-start(bf16[1,64,256]{2,1,0:T(8,128)(2,1)S(1)} %select_convert_fusion.6), channel_id=1, source_target_pairs={{0,8},{8,0},{16,24},{24,16},{1,9},{9,1},{17,25},{25,17},{2,10},{10... | collective-permute-start | bytes 98312 | tf_op jit(solution)/shard_map/ppermute | solution.py:14
  120.4 4.4 %collective-permute-start.5 = (bf16[2,64,256]{2,1,0:T(8,128)(2,1)S(1)}, bf16[2,64,256]{2,1,0:T(8,128)(2,1)S(1)}, u32[]{:S(2)}, u32[]{:S(2)}) collective-permute-start(bf16[2,64,256]{2,1,0:T(8,128)(2,1)S(1)} %select_convert_fusion.1), channel_id=1, source_target_pairs={{0,16},{8,24},{16,0},{24,8},{1,17},{9,25},{17,1},{25,9},{2,18},{10... | collective-permute-start | bytes 196616 | tf_op jit(solution)/shard_map/ppermute | solution.py:14
  124.8 4.0 %collective-permute-start.6 = (bf16[1,64,256]{2,1,0:T(8,128)(2,1)S(1)}, bf16[1,64,256]{2,1,0:T(8,128)(2,1)S(1)}, u32[]{:S(2)}, u32[]{:S(2)}) collective-permute-start(bf16[1,64,256]{2,1,0:T(8,128)(2,1)S(1)} %select_convert_fusion.5), channel_id=1, source_target_pairs={{0,8},{8,0},{16,24},{24,16},{1,9},{9,1},{17,25},{25,17},{2,10},{10... | collective-permute-start | bytes 98312 | tf_op jit(solution)/shard_map/ppermute | solution.py:14
  145.7 4.4 %collective-permute-start.7 = (bf16[2,64,256]{2,1,0:T(8,128)(2,1)S(1)}, bf16[2,64,256]{2,1,0:T(8,128)(2,1)S(1)}, u32[]{:S(2)}, u32[]{:S(2)}) collective-permute-start(bf16[2,64,256]{2,1,0:T(8,128)(2,1)S(1)} %select_convert_fusion), channel_id=1, source_target_pairs={{0,16},{8,24},{16,0},{24,8},{1,17},{9,25},{17,1},{25,9},{2,18},{10... | collective-permute-start | bytes 196616 | tf_op jit(solution)/shard_map/ppermute | solution.py:14
  150.2 4.0 %collective-permute-start.8 = (bf16[1,64,256]{2,1,0:T(8,128)(2,1)S(1)}, bf16[1,64,256]{2,1,0:T(8,128)(2,1)S(1)}, u32[]{:S(2)}, u32[]{:S(2)}) collective-permute-start(bf16[1,64,256]{2,1,0:T(8,128)(2,1)S(1)} %select_convert_fusion.4), channel_id=1, source_target_pairs={{0,8},{8,0},{16,24},{24,16},{1,9},{9,1},{17,25},{25,17},{2,10},{10... | collective-permute-start | bytes 98312 | tf_op jit(solution)/shard_map/ppermute | solution.py:14
  169.9 4.0 %collective-permute-start.9 = (bf16[1,64,256]{2,1,0:T(8,128)(2,1)S(1)}, bf16[1,64,256]{2,1,0:T(8,128)(2,1)S(1)}, u32[]{:S(2)}, u32[]{:S(2)}) collective-permute-start(bf16[1,64,256]{2,1,0:T(8,128)(2,1)S(1)} %fusion.23), channel_id=1, source_target_pairs={{0,8},{8,0},{16,24},{24,16},{1,9},{9,1},{17,25},{25,17},{2,10},{10... | collective-permute-start | bytes 98312 | tf_op jit(solution)/shard_map/ppermute | solution.py:14
  173.9 4.3 %collective-permute-start.10 = (bf16[2,64,256]{2,1,0:T(8,128)(2,1)S(1)}, bf16[2,64,256]{2,1,0:T(8,128)(2,1)S(1)}, u32[]{:S(2)}, u32[]{:S(2)}) collective-permute-start(bf16[2,64,256]{2,1,0:T(8,128)(2,1)S(1)} %maximum_select_fusion.4), channel_id=1, source_target_pairs={{0,16},{8,24},{16,0},{24,8},{1,17},{9,25},{17,1},{25,9},{2,18},{10... | collective-permute-start | bytes 196616 | tf_op jit(solution)/shard_map/ppermute | solution.py:14
  179.3 72.7 %all-gather.13.cloned.1.call-start = ((), (), s32[]{:S(2)}) async-start(), calls=%async_computation.1 | async-start | bytes 2359296 | tf_op jit(solution)/shard_map/all_gather | solution.py:8
  213.9 4.0 %collective-permute-start.11 = (bf16[1,64,256]{2,1,0:T(8,128)(2,1)S(1)}, bf16[1,64,256]{2,1,0:T(8,128)(2,1)S(1)}, u32[]{:S(2)}, u32[]{:S(2)}) collective-permute-start(bf16[1,64,256]{2,1,0:T(8,128)(2,1)S(1)} %fusion.22), channel_id=1, source_target_pairs={{0,8},{8,0},{16,24},{24,16},{1,9},{9,1},{17,25},{25,17},{2,10},{10... | collective-permute-start | bytes 98312 | tf_op jit(solution)/shard_map/ppermute | solution.py:14
  217.9 4.3 %collective-permute-start.12 = (bf16[2,64,256]{2,1,0:T(8,128)(2,1)S(1)}, bf16[2,64,256]{2,1,0:T(8,128)(2,1)S(1)}, u32[]{:S(2)}, u32[]{:S(2)}) collective-permute-start(bf16[2,64,256]{2,1,0:T(8,128)(2,1)S(1)} %maximum_select_fusion.5), channel_id=1, source_target_pairs={{0,16},{8,24},{16,0},{24,8},{1,17},{9,25},{17,1},{25,9},{2,18},{10... | collective-permute-start | bytes 196616 | tf_op jit(solution)/shard_map/ppermute | solution.py:14
  223.4 72.3 %all-gather.15.cloned.1.call-start = ((), (), s32[]{:S(2)}) async-start(), calls=%async_computation.2 | async-start | bytes 2359296 | tf_op jit(solution)/shard_map/all_gather | solution.py:8
  257.4 4.0 %collective-permute-start.13 = (bf16[1,64,256]{2,1,0:T(8,128)(2,1)S(1)}, bf16[1,64,256]{2,1,0:T(8,128)(2,1)S(1)}, u32[]{:S(2)}, u32[]{:S(2)}) collective-permute-start(bf16[1,64,256]{2,1,0:T(8,128)(2,1)S(1)} %fusion.21), channel_id=1, source_target_pairs={{0,8},{8,0},{16,24},{24,16},{1,9},{9,1},{17,25},{25,17},{2,10},{10... | collective-permute-start | bytes 98312 | tf_op jit(solution)/shard_map/ppermute | solution.py:14
  261.4 4.3 %collective-permute-start.14 = (bf16[2,64,256]{2,1,0:T(8,128)(2,1)S(1)}, bf16[2,64,256]{2,1,0:T(8,128)(2,1)S(1)}, u32[]{:S(2)}, u32[]{:S(2)}) collective-permute-start(bf16[2,64,256]{2,1,0:T(8,128)(2,1)S(1)} %maximum_select_fusion.6), channel_id=1, source_target_pairs={{0,16},{8,24},{16,0},{24,8},{1,17},{9,25},{17,1},{25,9},{2,18},{10... | collective-permute-start | bytes 196616 | tf_op jit(solution)/shard_map/ppermute | solution.py:14
  266.9 72.3 %all-gather.17.cloned.1.call-start = ((), (), s32[]{:S(2)}) async-start(), calls=%async_computation.3 | async-start | bytes 2359296 | tf_op jit(solution)/shard_map/all_gather | solution.py:8
  300.9 4.0 %collective-permute-start.15 = (bf16[1,64,256]{2,1,0:T(8,128)(2,1)S(1)}, bf16[1,64,256]{2,1,0:T(8,128)(2,1)S(1)}, u32[]{:S(2)}, u32[]{:S(2)}) collective-permute-start(bf16[1,64,256]{2,1,0:T(8,128)(2,1)S(1)} %fusion.20), channel_id=1, source_target_pairs={{0,8},{8,0},{16,24},{24,16},{1,9},{9,1},{17,25},{25,17},{2,10},{10... | collective-permute-start | bytes 98312 | tf_op jit(solution)/shard_map/ppermute | solution.py:14
  304.9 4.3 %collective-permute-start.16 = (bf16[2,64,256]{2,1,0:T(8,128)(2,1)S(1)}, bf16[2,64,256]{2,1,0:T(8,128)(2,1)S(1)}, u32[]{:S(2)}, u32[]{:S(2)}) collective-permute-start(bf16[2,64,256]{2,1,0:T(8,128)(2,1)S(1)} %maximum_select_fusion.7), channel_id=1, source_target_pairs={{0,16},{8,24},{16,0},{24,8},{1,17},{9,25},{17,1},{25,9},{2,18},{10... | collective-permute-start | bytes 196616 | tf_op jit(solution)/shard_map/ppermute | solution.py:14
  310.6 68.1 %all-gather.19.cloned.1.call-start = ((), (), s32[]{:S(2)}) async-start(), calls=%async_computation.4 | async-start | bytes 2359296 | tf_op jit(solution)/shard_map/all_gather | solution.py:8
  344.5 4.0 %collective-permute-start.17 = (bf16[1,64,256]{2,1,0:T(8,128)(2,1)S(1)}, bf16[1,64,256]{2,1,0:T(8,128)(2,1)S(1)}, u32[]{:S(2)}, u32[]{:S(2)}) collective-permute-start(bf16[1,64,256]{2,1,0:T(8,128)(2,1)S(1)} %fusion.19), channel_id=1, source_target_pairs={{0,8},{8,0},{16,24},{24,16},{1,9},{9,1},{17,25},{25,17},{2,10},{10... | collective-permute-start | bytes 98312 | tf_op jit(solution)/shard_map/ppermute | solution.py:14
  (29 other events, 236.9 us)
Sparse Core Ops, SparseCore 0:
  179.5 30.0 all-gather.10
  223.5 28.5 all-gather.12
  267.0 28.5 all-gather.14
  310.7 28.5 all-gather.16
  350.1 28.5 all-gather.18
